TPU v7x, 256 devices: a whole 4x4x8 slice. The times are simulated.
256 devices in a mesh: ma: 64 (over x, z, core), lev: 4 (over y).
Axes of the slice: x: 4, y: 4, z: 8, core: 2. Of those that a mesh axis runs over, the one named last changes fastest.
Arguments:
- forcing: float32 [72, 2, 1280, 1280], P('lev', None, 'ma'), may hold values from -80 to 80
- coupling: float32 [4, 1280, 1280], P(None, 'ma'), may hold values from -0.3 to 0.3
- helmholtz: float32 [1280], replicated, may hold values from 0.5 to 5
- vertical: float32 [72, 72], replicated, may hold values from -1 to 3, as said below
Outputs:
- solution: float32 [72, 2, 1280, 1280], P('lev', None, 'ma')
- norms: float32 [2], replicated
Inputs may be any that keep to these rules, and one draw needn't show every extreme that they name: `vertical`: the diagonal entries lie between 1 and 3.
All inputs are finite; a program needn't handle non-finite values.
Results may differ from a plain program's by a relative error of at most 0.000071.
Values sent between devices are 32-bit elements; how exact they have to be, the bound alone decides.
No kernel may reach another device: no remote copies, remote signals or barrier semaphores. Data moves between devices by JAX's collectives and lax.ppermute only.
A program may use at most 192 MiB of HBM per device.

v0:
```python
import jax
import jax.numpy as jnp
from jax import lax
from jax.sharding import Mesh
from jax.sharding import PartitionSpec as P

LEV = 72
WAVES = 1280
MA = ("ma_0", "ma_1", "ma_2")
MA_LEV = ("ma_0", "ma_1", "ma_2", "lev")
OFFSETS = (-2, -1, 1, 2)


def shifted(block, axis, distance):
    devices = range(lax.axis_size(axis))
    route = [(i - distance, i) for i in devices if i - distance in devices]
    return lax.ppermute(block, axis, route)


def by_axis(x, axes):
    for axis in axes:
        x = lax.psum(x, axis)
    return x


def owned_waves(rows, owners, index):
    fold = jnp.arange(rows, dtype=jnp.int32)
    return fold * owners + jnp.where(fold % 2 == 0, index, owners - 1 - index)


def next_row(block, direction):
    empty = jnp.zeros_like(block[:, :, :1])
    if direction > 0:
        return jnp.concatenate([block[:, :, 1:], empty], axis=2)
    return jnp.concatenate([empty, block[:, :, :-1]], axis=2)


def coupled(nearby, offset, owners, index, rows):
    fold = jnp.arange(rows, dtype=jnp.int32)
    even_fold = fold % 2 == 0
    source = jnp.where(even_fold, index + offset, index - offset)
    inside = (source >= 0) & (source < owners)
    upper = 2 * owners - 1 - 2 * index
    lower = -1 - 2 * index
    beyond = jnp.where(
        even_fold,
        jnp.where(source >= owners, upper - offset, lower - offset),
        jnp.where(source < 0, lower + offset, upper + offset),
    )
    picked = jnp.where(even_fold[None, None, :, None], nearby[offset], nearby[-offset])
    result = picked * inside.astype(jnp.float32)[None, None, :, None]
    direction = 1 if offset > 0 else -1
    for delta in (-1, 0, 1):
        weight = (~inside & (beyond == delta)).astype(jnp.float32)
        result = result + next_row(nearby[delta], direction) * weight[None, None, :, None]
    return result


def square_neighbours(values):
    nearby = {0: values}
    for distance in (1, 2, -1, -2):
        nearby[-distance] = shifted(values, MA, distance)
    return nearby


def norm_total(value):
    return by_axis(value, MA_LEV)


def body(forcing, coupling, helmholtz, vertical):
    owners = lax.axis_size(MA)
    index = lax.axis_index(MA)
    rows = forcing.shape[2]
    waves = owned_waves(rows, owners, index)
    width = forcing.shape[3]
    levels = forcing.shape[0]
    weights = lax.dynamic_slice_in_dim(vertical, lax.axis_index("lev") * levels, levels, 0)
    diagonal = lax.dynamic_slice_in_dim(
        jnp.diagonal(vertical), lax.axis_index("lev") * levels, levels, 0
    )
    positions = jnp.arange(width, dtype=jnp.int32)
    live = (positions[None, :] >= waves[:, None]).astype(jnp.float32)[None, None]
    scale = (1.0 / (1.0 + helmholtz[None, :] * diagonal[:, None]))[:, None, None, :]
    rhs = forcing * live
    first_sum = norm_total(jnp.sum(rhs * rhs))
    first = scale * rhs
    mixed = jnp.einsum(
        "kl,lcin->kcin",
        weights,
        lax.all_gather(first, "lev", axis=0, tiled=True),
        precision=lax.Precision.HIGHEST,
    )
    nearby = square_neighbours(first)
    result = first + helmholtz[None, None, None, :] * mixed
    for place, offset in enumerate(OFFSETS):
        result = result + coupling[place][None, None] * coupled(nearby, offset, owners, index, rows)
    residual = rhs - result * live
    solution = first + scale * residual
    second_sum = norm_total(jnp.sum(residual * residual))
    count = LEV * WAVES * (WAVES + 1)
    norms = jnp.sqrt(jnp.stack([first_sum, second_sum]) / count)
    return (solution, norms)


def solution(mesh):
    split = Mesh(mesh.devices.reshape(4, 8, 2, mesh.shape["lev"]), ("ma_0", "ma_1", "ma_2", "lev"))
    return jax.shard_map(
        body,
        mesh=split,
        in_specs=(P("lev", None, MA, None), P(None, MA, None), P(), P()),
        out_specs=(P("lev", None, MA, None), P()),
        check_vma=False,
    )
```

profile of v0, /device:TPU:1, one launch (start us, length us, event | category | flops | bytes accessed | tf_op | source)
XLA Modules:
  0.0 245.4 jit_solution(4459062973413210070)
XLA Ops:
  7.9 1.7 gather_fusion
  10.5 3.3 %fusion.19 = f32[18,2,20,1280]{3,0,2,1:T(8,128)S(1)} fusion(f32[18,2,20,1280]{3,1,2,0:T(2,128)} %param.4, f32[20,1280]{1,0:T(8,128)S(1)} %fusion.23, f32[18,1280]{1,0:T(8,128)S(1)} %add_divide_fusion), kind=kLoop, calls=%fused_computation.23 | loop fusion | flops 1843200 | bytes 7567360 | tf_op jit(solution)/shard_map/mul | solution.py:86
  13.8 2.2 copy-done.1
  16.0 4.7 %copy.15 = f32[18,2,20,1280]{3,1,2,0:T(2,128)} copy(f32[18,2,20,1280]{3,0,2,1:T(8,128)S(1)} %fusion.19) | data formatting | bytes 7372800 | tf_op jit(solution)/shard_map/mul | solution.py:86
  20.7 5.2 %collective-permute-start.3 = (f32[18,2,20,1280]{3,1,2,0:T(2,128)}, f32[18,2,20,1280]{3,1,2,0:T(2,128)}, u32[]{:S(2)}, u32[]{:S(2)}) collective-permute-start(f32[18,2,20,1280]{3,1,2,0:T(2,128)} %copy.15), channel_id=1, source_target_pairs={{4,0},{8,4},{12,8},{16,12},{20,16},{24,20},{28,24},{32,28},{36,32}... | collective-permute-start | bytes 11059208 | tf_op jit(solution)/shard_map/ppermute | solution.py:17
  25.8 1.9 collective-permute-start.2
  29.1 5.9 %collective-permute-start = (f32[18,2,20,1280]{3,1,2,0:T(2,128)}, f32[18,2,20,1280]{3,1,2,0:T(2,128)}, u32[]{:S(2)}, u32[]{:S(2)}) collective-permute-start(f32[18,2,20,1280]{3,1,2,0:T(2,128)} %copy.15), channel_id=1, source_target_pairs={{0,8},{4,12},{8,16},{12,20},{16,24},{20,28},{24,32},{28,36},{32,40... | collective-permute-start | bytes 11059208 | tf_op jit(solution)/shard_map/ppermute | solution.py:17
  35.5 9.8 %fusion.41 = (f32[18,2,19,1280]{3,0,2,1:T(8,128)}, f32[18,2,19,1280]{3,0,2,1:T(8,128)}) fusion(f32[18,2,20,1280]{3,0,2,1:T(8,128)} %copy-done.1), kind=kLoop, calls=%fused_computation.75 | loop fusion | bytes 14008320 | tf_op jit(solution)/shard_map/slice | solution.py:35
  45.2 53.9 %collective-permute-done.2 = f32[18,2,20,1280]{3,1,2,0:T(2,128)} collective-permute-done((f32[18,2,20,1280]{3,1,2,0:T(2,128)}, f32[18,2,20,1280]{3,1,2,0:T(2,128)}, u32[]{:S(2)}, u32[]{:S(2)}) %collective-permute-start.2) | collective-permute-done | bytes 3686432 | tf_op jit(solution)/shard_map/ppermute | solution.py:17
  99.1 5.6 %fusion.42 = (f32[18,2,19,1280]{3,1,2,0:T(2,128)S(1)}, f32[18,2,19,1280]{3,1,2,0:T(2,128)S(1)}) fusion(f32[18,2,20,1280]{3,1,2,0:T(2,128)} %collective-permute-done.2), kind=kLoop, calls=%fused_computation.76 | loop fusion | bytes 14008320 | tf_op jit(solution)/shard_map/slice | solution.py:35
  104.6 2.5 %copy.141 = f32[18,2,19,1280]{3,0,2,1:T(8,128)} copy(f32[18,2,19,1280]{3,1,2,0:T(2,128)S(1)} %get-tuple-element.37) | data formatting | bytes 7004160
  107.1 2.6 %copy.139 = f32[18,2,19,1280]{3,0,2,1:T(8,128)} copy(f32[18,2,19,1280]{3,1,2,0:T(2,128)S(1)} %get-tuple-element.38) | data formatting | bytes 7004160
  109.8 5.5 %fusion.43 = (f32[18,2,19,1280]{3,1,2,0:T(2,128)S(1)}, f32[18,2,19,1280]{3,1,2,0:T(2,128)S(1)}) fusion(f32[18,2,20,1280]{3,1,2,0:T(2,128)} %collective-permute-done.3), kind=kLoop, calls=%fused_computation.77 | loop fusion | bytes 14008320 | tf_op jit(solution)/shard_map/slice | solution.py:35
  115.2 2.5 %copy.140 = f32[18,2,19,1280]{3,0,2,1:T(8,128)} copy(f32[18,2,19,1280]{3,1,2,0:T(2,128)S(1)} %get-tuple-element.39) | data formatting | bytes 7004160
  117.7 2.5 %copy.138 = f32[18,2,19,1280]{3,0,2,1:T(8,128)} copy(f32[18,2,19,1280]{3,1,2,0:T(2,128)S(1)} %get-tuple-element.40) | data formatting | bytes 7004160
  120.2 26.9 %collective-permute-done = f32[18,2,20,1280]{3,1,2,0:T(2,128)} collective-permute-done((f32[18,2,20,1280]{3,1,2,0:T(2,128)}, f32[18,2,20,1280]{3,1,2,0:T(2,128)}, u32[]{:S(2)}, u32[]{:S(2)}) %collective-permute-start) | collective-permute-done | bytes 3686432 | tf_op jit(solution)/shard_map/ppermute | solution.py:17
  147.1 17.0 %all-gather.2.cloned.1.call-done = f32[72,2,20,1280]{3,1,2,0:T(2,128)} async-done(((f32[18,2,20,1280]{3,1,2,0:T(2,128)}), f32[72,2,20,1280]{3,1,2,0:T(2,128)}) %all-gather.2.cloned.1.call-update) | async-done | bytes 14745616 | tf_op jit(solution)/shard_map/all_gather | solution.py:90
  164.1 27.1 %multiply_reduce_fusion = (f32[]{:T(128)}, f32[18,2,20,1280]{3,0,2,1:T(8,128)S(1)}, f32[]{:T(128)}) fusion(f32[20,1280]{1,0:T(8,128)S(1)} %fusion.23, f32[18,2,20,1280]{3,1,2,0:T(2,128)} %param.4, f32[18,1280]{1,0:T(8,128)S(1)} %add_divide_fusion, f32[20]{0:T(128)S(1)} %get-tuple-element.52, f32[20]{0:T(128)S(1)} %get-tuple-element.51, ...), kind=kOutput, calls=%fused_computation.25 | convolution fusion | flops 844185600 | bytes 58642956 | tf_op jit(solution)/shard_map/kl,lcin->kcin/dot_general | solution.py:87
  191.2 4.7 %copy.37 = f32[18,2,20,1280]{3,1,2,0:T(2,128)} copy(f32[18,2,20,1280]{3,0,2,1:T(8,128)S(1)} %get-tuple-element.33) | data formatting | bytes 7372800
  195.9 9.0 %all-reduce.8 = (f32[]{:T(128)}, f32[]{:T(128)}) all-reduce(f32[]{:T(128)} %get-tuple-element.32, f32[]{:T(128)} %get-tuple-element.36), channel_id=1, replica_groups=mesh['ma_0'=4,'ma_1'=8,'ma_2'=2,'lev'=4] {'ma_0'}, use_global_device_ids=true, to_apply=%region_6.7 | all-reduce | flops 2 | bytes 16 | tf_op jit(solution)/shard_map/psum | solution.py:22
  204.9 14.4 %all-reduce.6 = (f32[]{:T(128)}, f32[]{:T(128)}) all-reduce(f32[]{:T(128)} %get-tuple-element.12, f32[]{:T(128)} %get-tuple-element.13), channel_id=1, replica_groups=mesh['ma_0'=4,'ma_1'=8,'ma_2'=2,'lev'=4] {'ma_1'}, use_global_device_ids=true, to_apply=%region_7.8 | all-reduce | flops 2 | bytes 16 | tf_op jit(solution)/shard_map/psum | solution.py:22
  219.3 9.2 %all-reduce.9 = (f32[]{:T(128)}, f32[]{:T(128)}) all-reduce(f32[]{:T(128)} %get-tuple-element.8, f32[]{:T(128)} %get-tuple-element.9), channel_id=1, replica_groups=mesh['ma_0'=4,'ma_1'=8,'ma_2'=2,'lev'=4] {'ma_2'}, use_global_device_ids=true, to_apply=%region_8.9 | all-reduce | flops 2 | bytes 16 | tf_op jit(solution)/shard_map/psum | solution.py:22
  228.5 8.1 %all-reduce.7 = (f32[1]{0:T(128)}, f32[1]{0:T(128)}) all-reduce(f32[1]{0:T(128)} %bitcast.8, f32[1]{0:T(128)} %bitcast.7), channel_id=1, replica_groups=mesh['ma_0'=4,'ma_1'=8,'ma_2'=2,'lev'=4] {'lev'}, use_global_device_ids=true, to_apply=%region_9.10 | all-reduce | flops 2 | bytes 16 | tf_op jit(solution)/shard_map/psum | solution.py:22
  236.7 1.8 fusion.31
  (31 shorter events, 3.4 us)
Async XLA Ops:
  7.2 0.8 copy-start
  7.2 156.9 %all-gather.2.cloned.1.call-start = ((), (), s32[]{:S(2)}) async-start(), calls=%async_computation | async-start | bytes 18432000 | tf_op jit(solution)/shard_map/all_gather | solution.py:90
  13.8 2.2 copy-start.1
  16.0 19.1 %copy-start.2 = (f32[4,20,1280]{2,0,1:T(4,128)S(1)}, f32[4,20,1280]{2,0,1:T(4,128)}, u32[]{:S(2)}) copy-start(f32[4,20,1280]{2,0,1:T(4,128)} %param.5) | copy-start | bytes 1228804
  20.7 89.1 %collective-permute-start.3 = (f32[18,2,20,1280]{3,1,2,0:T(2,128)}, f32[18,2,20,1280]{3,1,2,0:T(2,128)}, u32[]{:S(2)}, u32[]{:S(2)}) collective-permute-start(f32[18,2,20,1280]{3,1,2,0:T(2,128)} %copy.15), channel_id=1, source_target_pairs={{4,0},{8,4},{12,8},{16,12},{20,16},{24,20},{28,24},{32,28},{36,32}... | collective-permute-start | bytes 11059208 | tf_op jit(solution)/shard_map/ppermute | solution.py:17
  25.8 73.2 %collective-permute-start.2 = (f32[18,2,20,1280]{3,1,2,0:T(2,128)}, f32[18,2,20,1280]{3,1,2,0:T(2,128)}, u32[]{:S(2)}, u32[]{:S(2)}) collective-permute-start(f32[18,2,20,1280]{3,1,2,0:T(2,128)} %copy.15), channel_id=1, source_target_pairs={{0,4},{4,8},{8,12},{12,16},{16,20},{20,24},{24,28},{28,32},{32,36}... | collective-permute-start | bytes 11059208 | tf_op jit(solution)/shard_map/ppermute | solution.py:17
  27.8 92.4 %collective-permute-start.1 = (f32[18,2,20,1280]{3,1,2,0:T(2,128)}, f32[18,2,20,1280]{3,1,2,0:T(2,128)}, u32[]{:S(2)}, u32[]{:S(2)}) collective-permute-start(f32[18,2,20,1280]{3,1,2,0:T(2,128)} %copy.15), channel_id=1, source_target_pairs={{8,0},{12,4},{16,8},{20,12},{24,16},{28,20},{32,24},{36,28},{40,32... | collective-permute-start | bytes 11059208 | tf_op jit(solution)/shard_map/ppermute | solution.py:17
  29.1 118.0 %collective-permute-start = (f32[18,2,20,1280]{3,1,2,0:T(2,128)}, f32[18,2,20,1280]{3,1,2,0:T(2,128)}, u32[]{:S(2)}, u32[]{:S(2)}) collective-permute-start(f32[18,2,20,1280]{3,1,2,0:T(2,128)} %copy.15), channel_id=1, source_target_pairs={{0,8},{4,12},{8,16},{12,20},{16,24},{20,28},{24,32},{28,36},{32,40... | collective-permute-start | bytes 11059208 | tf_op jit(solution)/shard_map/ppermute | solution.py:17
  117.7 46.4 %copy-start.3 = (f32[1280]{0:T(1024)S(1)}, f32[1280]{0:T(1024)}, u32[]{:S(2)}) copy-start(f32[1280]{0:T(1024)} %param.6) | copy-start | bytes 15364
Sparse Core Ops, SparseCore 0:
  20.8 143.2 all-gather.1
where the time goes:
time: 246 us; the launch traced here: 245 us
  waiting for transfers between devices  97.8 us (40%)
  local copies, waits for them, and re-layouts  45.2 us (18%)
  blocking collectives  40.8 us (17%)
  matrix products  27.1 us (11%)
  starting transfers between devices  14.3 us (6%)
  between operations  14.2 us (6%)
  other arithmetic  6.09 us (2%)
    ppermute x4, waiting for transfers between devices, shifted(): return lax.ppermute(block, axis, route)  80.7 us
    psum x4, blocking collectives, by_axis(): x = lax.psum(x, axis)  40.8 us
    dot_general x1, matrix products, body(): jnp.einsum('kl,lcin->kcin', weights, lax.all_gather(first, 'lev', axis=0,...  27.1 us
    slice x3, local copies, waits for them, and re-layouts, next_row(): return jnp.concatenate([empty, block[:, :, :-1]], axis=2)  20.8 us
    unnamed x13, local copies, waits for them, and re-layouts  17.6 us
    all_gather x1, waiting for transfers between devices, body(): lax.all_gather(first, 'lev', axis=0, tiled=True)  17 us
    ppermute x4, starting transfers between devices, shifted(): return lax.ppermute(block, axis, route)  14.2 us
  transfers between devices with their start and end apart: 5, of which 3 were waited for; matrix products, arithmetic and copies ran while one was open for 13% of the time, Pallas kernels for 0%

commit v1 on v0

--- a/solution.py
+++ b/solution.py
@@ -19,7 +19,7 @@
 
 def by_axis(x, axes):
     for axis in axes:
-        x = lax.psum(x, axis)
+        x = jnp.sum(lax.all_gather(x, axis), axis=0)
     return x
 
 

time: 246 us -> 267 us (1.085)
  local copies, waits for them, and re-layouts: 45.2 us -> 61.4 us
  other arithmetic: 6.09 us -> 11.2 us
  matrix products: 27.1 us -> 30.3 us
  blocking collectives: 40.8 us -> 38 us
    psum x4 -> x0, blocking collectives: 40.8 us -> none  [by_axis(): x = lax.psum(x, axis)]
    unnamed x0 -> x4, blocking collectives: none -> 38 us
    unnamed x13 -> x41, local copies, waits for them, and re-layouts: 17.6 us -> 33.7 us
    reduce_sum x0 -> x8, other arithmetic: none -> 5.12 us  [by_axis(): x = jnp.sum(lax.all_gather(x, axis), axis=0)]
    dot_general x1, matrix products: 27.1 us -> 30.3 us  [body(): jnp.einsum('kl,lcin->kcin', weights, lax.all_gather(first, 'lev', axis=0,...]
  transfers between devices with their start and end apart: 5 -> 5, of which waited for: 3 -> 3; matrix products, arithmetic and copies ran while one was open for 13% -> 12% of each run, Pallas kernels for 0% -> 0%
where the time goes in v1:
time: 267 us; the launch traced here: 266 us
  waiting for transfers between devices  97.5 us (37%)
  local copies, waits for them, and re-layouts  61.4 us (23%)
  blocking collectives  38 us (14%)
  matrix products  30.3 us (11%)
  between operations  14.3 us (5%)
  starting transfers between devices  13.7 us (5%)
  other arithmetic  11.2 us (4%)
    ppermute x4, waiting for transfers between devices, shifted(): return lax.ppermute(block, axis, route)  80.5 us
    unnamed x4, blocking collectives  38 us
    unnamed x41, local copies, waits for them, and re-layouts  33.7 us
    dot_general x1, matrix products, body(): jnp.einsum('kl,lcin->kcin', weights, lax.all_gather(first, 'lev', axis=0,...  30.3 us
    slice x3, local copies, waits for them, and re-layouts, next_row(): return jnp.concatenate([empty, block[:, :, :-1]], axis=2)  20.9 us
    all_gather x1, waiting for transfers between devices, body(): lax.all_gather(first, 'lev', axis=0, tiled=True)  17 us
    ppermute x4, starting transfers between devices, shifted(): return lax.ppermute(block, axis, route)  13.7 us
  transfers between devices with their start and end apart: 5, of which 3 were waited for; matrix products, arithmetic and copies ran while one was open for 12% of the time, Pallas kernels for 0%

profile of v1, /device:TPU:1, one launch (start us, length us, event | category | flops | bytes accessed | tf_op | source)
XLA Modules:
  0.0 266.3 jit_solution(6246355684944484087)
XLA Ops:
  7.9 1.7 gather_fusion
  10.5 3.3 %fusion.19 = f32[18,2,20,1280]{3,0,2,1:T(8,128)S(1)} fusion(f32[18,2,20,1280]{3,1,2,0:T(2,128)} %param.4, f32[20,1280]{1,0:T(8,128)S(1)} %fusion.23, f32[18,1280]{1,0:T(8,128)S(1)} %add_divide_fusion), kind=kLoop, calls=%fused_computation.23 | loop fusion | flops 1843200 | bytes 7567360 | tf_op jit(solution)/shard_map/mul | solution.py:86
  13.8 2.2 copy-done.1
  16.0 4.7 %copy.15 = f32[18,2,20,1280]{3,1,2,0:T(2,128)} copy(f32[18,2,20,1280]{3,0,2,1:T(8,128)S(1)} %fusion.19) | data formatting | bytes 7372800 | tf_op jit(solution)/shard_map/mul | solution.py:86
  20.7 5.2 %collective-permute-start.3 = (f32[18,2,20,1280]{3,1,2,0:T(2,128)}, f32[18,2,20,1280]{3,1,2,0:T(2,128)}, u32[]{:S(2)}, u32[]{:S(2)}) collective-permute-start(f32[18,2,20,1280]{3,1,2,0:T(2,128)} %copy.15), channel_id=1, source_target_pairs={{4,0},{8,4},{12,8},{16,12},{20,16},{24,20},{28,24},{32,28},{36,32}... | collective-permute-start | bytes 11059208 | tf_op jit(solution)/shard_map/ppermute | solution.py:17
  25.8 1.9 collective-permute-start.2
  27.7 5.1 %collective-permute-start = (f32[18,2,20,1280]{3,1,2,0:T(2,128)}, f32[18,2,20,1280]{3,1,2,0:T(2,128)}, u32[]{:S(2)}, u32[]{:S(2)}) collective-permute-start(f32[18,2,20,1280]{3,1,2,0:T(2,128)} %copy.15), channel_id=1, source_target_pairs={{0,8},{4,12},{8,16},{12,20},{16,24},{20,28},{24,32},{28,36},{32,40... | collective-permute-start | bytes 11059208 | tf_op jit(solution)/shard_map/ppermute | solution.py:17
  35.5 9.7 %fusion.41 = (f32[18,2,19,1280]{3,0,2,1:T(8,128)}, f32[18,2,19,1280]{3,0,2,1:T(8,128)}) fusion(f32[18,2,20,1280]{3,0,2,1:T(8,128)} %copy-done.1), kind=kLoop, calls=%fused_computation.75 | loop fusion | bytes 14008320 | tf_op jit(solution)/shard_map/slice | solution.py:35
  45.3 50.8 %collective-permute-done.3 = f32[18,2,20,1280]{3,1,2,0:T(2,128)} collective-permute-done((f32[18,2,20,1280]{3,1,2,0:T(2,128)}, f32[18,2,20,1280]{3,1,2,0:T(2,128)}, u32[]{:S(2)}, u32[]{:S(2)}) %collective-permute-start.3) | collective-permute-done | bytes 3686432 | tf_op jit(solution)/shard_map/ppermute | solution.py:17
  96.1 5.6 %fusion.43 = (f32[18,2,19,1280]{3,1,2,0:T(2,128)S(1)}, f32[18,2,19,1280]{3,1,2,0:T(2,128)S(1)}) fusion(f32[18,2,20,1280]{3,1,2,0:T(2,128)} %collective-permute-done.3), kind=kLoop, calls=%fused_computation.77 | loop fusion | bytes 14008320 | tf_op jit(solution)/shard_map/slice | solution.py:35
  101.6 2.5 copy.138
  104.1 5.6 %fusion.42 = (f32[18,2,19,1280]{3,1,2,0:T(2,128)S(1)}, f32[18,2,19,1280]{3,1,2,0:T(2,128)S(1)}) fusion(f32[18,2,20,1280]{3,1,2,0:T(2,128)} %collective-permute-done.2), kind=kLoop, calls=%fused_computation.76 | loop fusion | bytes 14008320 | tf_op jit(solution)/shard_map/slice | solution.py:35
  109.7 2.6 copy.139
  112.3 2.5 copy.140
  114.8 2.6 copy.141
  117.4 29.7 %collective-permute-done = f32[18,2,20,1280]{3,1,2,0:T(2,128)} collective-permute-done((f32[18,2,20,1280]{3,1,2,0:T(2,128)}, f32[18,2,20,1280]{3,1,2,0:T(2,128)}, u32[]{:S(2)}, u32[]{:S(2)}) %collective-permute-start) | collective-permute-done | bytes 3686432 | tf_op jit(solution)/shard_map/ppermute | solution.py:17
  147.1 17.0 %all-gather.2.cloned.1.call-done = f32[72,2,20,1280]{3,1,2,0:T(2,128)} async-done(((f32[18,2,20,1280]{3,1,2,0:T(2,128)}), f32[72,2,20,1280]{3,1,2,0:T(2,128)}) %all-gather.2.cloned.1.call-update) | async-done | bytes 14745616 | tf_op jit(solution)/shard_map/all_gather | solution.py:90
  164.1 30.3 %multiply_reduce_fusion = (f32[]{:T(128)}, f32[18,2,20,1280]{3,0,2,1:T(8,128)}, f32[]{:T(128)}) fusion(f32[20,1280]{1,0:T(8,128)S(1)} %fusion.23, f32[18,2,20,1280]{3,1,2,0:T(2,128)} %param.4, f32[18,1280]{1,0:T(8,128)S(1)} %add_divide_fusion, f32[20]{0:T(128)S(1)} %get-tuple-element.52, f32[20]{0:T(128)S(1)} %get-tuple-element.51, ...), kind=kOutput, calls=%fused_computation.25 | convolution fusion | flops 844185600 | bytes 58642956 | tf_op jit(solution)/shard_map/kl,lcin->kcin/dot_general | solution.py:87
  197.7 8.4 %all-reduce.16 = (f32[4]{0:T(128)S(1)}, f32[4]{0:T(128)S(1)}) all-reduce(f32[4]{0:T(128)S(1)} %dynamic-update-slice.4, f32[4]{0:T(128)S(1)} %dynamic-update-slice), channel_id=1, replica_groups=mesh['ma_0'=4,'ma_1'=8,'ma_2'=2,'lev'=4] {'ma_0'}, use_global_device_ids=true, to_apply=%add.10 | all-reduce | flops 8 | bytes 64
  210.8 13.7 %all-reduce.14 = (f32[8]{0:T(128)S(1)}, f32[8]{0:T(128)S(1)}) all-reduce(f32[8]{0:T(128)S(1)} %dynamic-update-slice.5, f32[8]{0:T(128)S(1)} %dynamic-update-slice.1), channel_id=1, replica_groups=mesh['ma_0'=4,'ma_1'=8,'ma_2'=2,'lev'=4] {'ma_1'}, use_global_device_ids=true, to_apply=%add.11 | all-reduce | flops 16 | bytes 128
  229.2 8.6 %all-reduce.17 = (f32[2]{0:T(128)S(1)}, f32[2]{0:T(128)S(1)}) all-reduce(f32[2]{0:T(128)S(1)} %dynamic-update-slice.6, f32[2]{0:T(128)S(1)} %dynamic-update-slice.2), channel_id=1, replica_groups=mesh['ma_0'=4,'ma_1'=8,'ma_2'=2,'lev'=4] {'ma_2'}, use_global_device_ids=true, to_apply=%add.12 | all-reduce | flops 4 | bytes 32
  241.9 7.1 %copy.37 = f32[18,2,20,1280]{3,1,2,0:T(2,128)} copy(f32[18,2,20,1280]{3,0,2,1:T(8,128)} %get-tuple-element.33) | data formatting | bytes 7372800
  248.9 7.4 %all-reduce.15 = (f32[4]{0:T(128)S(1)}, f32[4]{0:T(128)S(1)}) all-reduce(f32[4]{0:T(128)S(1)} %dynamic-update-slice.7, f32[4]{0:T(128)S(1)} %dynamic-update-slice.3), channel_id=1, replica_groups=mesh['ma_0'=4,'ma_1'=8,'ma_2'=2,'lev'=4] {'lev'}, use_global_device_ids=true, to_apply=%add.13 | all-reduce | flops 8 | bytes 64
  257.6 1.8 fusion.31
  (67 shorter events, 22.3 us)
Async XLA Ops:
  7.2 0.8 copy-start
  7.2 156.9 %all-gather.2.cloned.1.call-start = ((), (), s32[]{:S(2)}) async-start(), calls=%async_computation | async-start | bytes 18432000 | tf_op jit(solution)/shard_map/all_gather | solution.py:90
  13.8 2.2 copy-start.1
  15.9 18.6 %copy-start.7 = (u32[256]{0:T(256)S(1)}, u32[256]{0:T(256)}, u32[]{:S(2)}) copy-start(u32[256]{0:T(256)} %constant.143) | copy-start | bytes 3076
  15.9 19.2 %copy-start.2 = (f32[4,20,1280]{2,0,1:T(4,128)S(1)}, f32[4,20,1280]{2,0,1:T(4,128)}, u32[]{:S(2)}) copy-start(f32[4,20,1280]{2,0,1:T(4,128)} %param.5) | copy-start | bytes 1228804
  20.7 75.4 %collective-permute-start.3 = (f32[18,2,20,1280]{3,1,2,0:T(2,128)}, f32[18,2,20,1280]{3,1,2,0:T(2,128)}, u32[]{:S(2)}, u32[]{:S(2)}) collective-permute-start(f32[18,2,20,1280]{3,1,2,0:T(2,128)} %copy.15), channel_id=1, source_target_pairs={{4,0},{8,4},{12,8},{16,12},{20,16},{24,20},{28,24},{32,28},{36,32}... | collective-permute-start | bytes 11059208 | tf_op jit(solution)/shard_map/ppermute | solution.py:17
  25.8 78.3 %collective-permute-start.2 = (f32[18,2,20,1280]{3,1,2,0:T(2,128)}, f32[18,2,20,1280]{3,1,2,0:T(2,128)}, u32[]{:S(2)}, u32[]{:S(2)}) collective-permute-start(f32[18,2,20,1280]{3,1,2,0:T(2,128)} %copy.15), channel_id=1, source_target_pairs={{0,4},{4,8},{8,12},{12,16},{16,20},{20,24},{24,28},{28,32},{32,36}... | collective-permute-start | bytes 11059208 | tf_op jit(solution)/shard_map/ppermute | solution.py:17
  27.7 119.3 %collective-permute-start = (f32[18,2,20,1280]{3,1,2,0:T(2,128)}, f32[18,2,20,1280]{3,1,2,0:T(2,128)}, u32[]{:S(2)}, u32[]{:S(2)}) collective-permute-start(f32[18,2,20,1280]{3,1,2,0:T(2,128)} %copy.15), channel_id=1, source_target_pairs={{0,8},{4,12},{8,16},{12,20},{16,24},{20,28},{24,32},{28,36},{32,40... | collective-permute-start | bytes 11059208 | tf_op jit(solution)/shard_map/ppermute | solution.py:17
  32.9 114.2 %collective-permute-start.1 = (f32[18,2,20,1280]{3,1,2,0:T(2,128)}, f32[18,2,20,1280]{3,1,2,0:T(2,128)}, u32[]{:S(2)}, u32[]{:S(2)}) collective-permute-start(f32[18,2,20,1280]{3,1,2,0:T(2,128)} %copy.15), channel_id=1, source_target_pairs={{8,0},{12,4},{16,8},{20,12},{24,16},{28,20},{32,24},{36,28},{40,32... | collective-permute-start | bytes 11059208 | tf_op jit(solution)/shard_map/ppermute | solution.py:17
  114.8 49.3 %copy-start.3 = (f32[1280]{0:T(1024)S(1)}, f32[1280]{0:T(1024)}, u32[]{:S(2)}) copy-start(f32[1280]{0:T(1024)} %param.6) | copy-start | bytes 15364
  164.1 33.0 %copy-start.6 = (u32[256]{0:T(256)S(1)}, u32[256]{0:T(256)}, u32[]{:S(2)}) copy-start(u32[256]{0:T(256)} %constant.148) | copy-start | bytes 3076
  164.1 46.1 %copy-start.5 = (u32[256]{0:T(256)S(1)}, u32[256]{0:T(256)}, u32[]{:S(2)}) copy-start(u32[256]{0:T(256)} %constant.153) | copy-start | bytes 3076
  164.1 64.5 %copy-start.4 = (u32[256]{0:T(256)S(1)}, u32[256]{0:T(256)}, u32[]{:S(2)}) copy-start(u32[256]{0:T(256)} %constant.158) | copy-start | bytes 3076
Sparse Core Ops, SparseCore 0:
  20.8 143.2 all-gather.1
